TPU v7x, 32 devices: a whole 2x2x4 slice. The times are simulated.
32 devices in a mesh: groups: 2 (over y), space: 4 (over z), tm: 2 (over x), chan: 2 (over core).
Axes of the slice: x: 2, y: 2, z: 4, core: 2. Of those that a mesh axis runs over, the one named last changes fastest.
Arguments:
- hidden_states: bfloat16 [8, 4, 64, 512], P(('groups', 'tm'), 'space', None, 'chan'), parts along dimension 0, may hold values from -25 to 25
- first_gain: float32 [512], P('chan'), may hold values from 0.1 to 1.9
- second_gain: float32 [512], P('chan'), may hold values from 0.1 to 1.9
- query_weight: bfloat16 [512, 512], replicated, may hold values from -0.4861359 to 0.4861359
- key_weight: bfloat16 [512, 512], replicated, may hold values from -0.4861359 to 0.4861359
- value_weight: bfloat16 [512, 512], replicated, may hold values from -0.25 to 0.25
- out_weight: bfloat16 [512, 512], replicated, may hold values from -0.25 to 0.25
- conv_kernel: bfloat16 [3, 3, 3, 512, 512], P(None, None, None, 'tm', 'chan'), may hold values from -0.0546875 to 0.0546875
Outputs:
- attended: bfloat16 [8, 4, 64, 512], P(('groups', 'tm'), 'space', None, 'chan'), parts along dimension 0
- convolved: bfloat16 [8, 4, 64, 512], P(('groups', 'tm'), 'space', None, 'chan'), parts along dimension 0
There are 2 independent parts, one for each index of `groups`. A program takes and returns all parts, laid end to end along the dimension named above; an argument that names none is the same for every part. Nothing has to cross between parts.
All inputs are finite; a program needn't handle non-finite values.
Results may differ from a plain program's by a relative error of at most 0.012.
The roundings to bfloat16 on the way count: a program that leaves them out, or rounds other values in their place, can miss the bound.
Values may be sent and summed in bfloat16 or wider, within the bound.
A program may use at most 64 MiB of HBM per device.

v0:
```python
import jax
import jax.numpy as jnp
from jax import lax
from jax.sharding import PartitionSpec as P

D = 512
NGROUP = 32
EPSILON = 1e-06


def shifted_2(x, axis, by):
    peers = lax.axis_size(axis)
    pairs = [(i, i + by) for i in range(peers) if 0 <= i + by < peers]
    return lax.ppermute(x, axis, pairs)


def padded_2(cells, sides, width):
    for axis, dim in sides:
        count = lax.axis_size(axis)
        ends = count - 1
        head = lax.slice_in_dim(cells, 0, width, axis=dim)
        tail = lax.slice_in_dim(cells, cells.shape[dim] - width, cells.shape[dim], axis=dim)
        cells = jnp.concatenate(
            [
                lax.ppermute(tail, axis, [(i, (i + 1) % count) for i in range(ends)]),
                cells,
                lax.ppermute(head, axis, [((i + 1) % count, i) for i in range(ends)]),
            ],
            axis=dim,
        )
    return cells


def normalize(source, gain_vector):
    channels = source.shape[3]
    group_width = D // NGROUP
    grouped = source.reshape(-1, channels // group_width, group_width)
    population = grouped.shape[0] * group_width * lax.axis_size("space") * lax.axis_size("tm")
    group_sums, group_squares = lax.psum(
        (jnp.sum(grouped, axis=(0, 2)), jnp.sum(grouped * grouped, axis=(0, 2))), ("space", "tm")
    )
    centre = group_sums / population
    spread = jnp.maximum(group_squares / population - centre * centre, 0.0)
    shifted = grouped - centre[None, :, None]
    scaled = shifted * lax.rsqrt(spread + EPSILON)[None, :, None]
    return scaled.reshape(source.shape) * gain_vector


def attend(normed, query_weight, key_weight, value_weight, out_weight):
    frame_count, row_count, col_count, channels = normed.shape
    token_count = frame_count * row_count * col_count
    tokens = normed.reshape(token_count, channels)
    halves = lax.all_to_all(tokens, "chan", split_axis=0, concat_axis=1, tiled=True)
    half_rows = halves.shape[0]
    queries = jnp.dot(halves, query_weight, preferred_element_type=jnp.float32).astype(jnp.bfloat16)
    keyed = jnp.dot(halves, key_weight, preferred_element_type=jnp.float32).astype(jnp.bfloat16)
    valued = jnp.dot(halves, value_weight, preferred_element_type=jnp.float32).astype(jnp.bfloat16)
    score_scale = D ** (-0.5)
    running_max = jnp.full((half_rows,), -1e30, jnp.float32)
    key_piece = lax.all_gather(keyed, "space", axis=0, tiled=True)
    value_piece = lax.all_gather(valued, "space", axis=0, tiled=True)
    scores = jnp.dot(queries, key_piece.T, preferred_element_type=jnp.float32) * score_scale
    newest_max = jnp.maximum(running_max, jnp.max(scores, axis=1))
    weights = jnp.exp(scores - newest_max[:, None])
    running_sum = jnp.sum(weights, axis=1)
    accumulated = jnp.dot(
        weights.astype(jnp.bfloat16), value_piece, preferred_element_type=jnp.float32
    )
    mixed = (accumulated / running_sum[:, None]).astype(jnp.bfloat16)
    projected = jnp.dot(mixed, out_weight, preferred_element_type=jnp.float32).astype(jnp.bfloat16)
    returned = lax.all_to_all(projected, "chan", split_axis=1, concat_axis=0, tiled=True)
    return returned.reshape(frame_count, row_count, col_count, channels)


def join_channels(activated):
    return lax.all_gather(activated, "chan", axis=3, tiled=True)


def extend(frames_in):
    earlier = shifted_2(frames_in, "tm", 1)
    timed = jnp.concatenate([earlier, frames_in], axis=0)
    rimmed = padded_2(timed, (("space", 1),), 1)
    return jnp.pad(rimmed, ((0, 0), (0, 0), (1, 1), (0, 0)))


def convolve(activated, conv_kernel):
    frame_count, row_count, col_count = (activated.shape[0], activated.shape[1], activated.shape[2])
    padded = extend(join_channels(activated))
    out_width = conv_kernel.shape[4]
    initial = jnp.zeros((frame_count * row_count * col_count, out_width), jnp.float32)
    running_total = initial
    piece = lax.all_gather(conv_kernel, "tm", axis=3, tiled=True)
    for time_tap in range(3):
        for row_tap in range(3):
            for col_tap in range(3):
                window = padded[
                    time_tap : time_tap + frame_count,
                    row_tap : row_tap + row_count,
                    col_tap : col_tap + col_count,
                ]
                window = window.reshape(frame_count * row_count * col_count, piece.shape[3])
                running_total = running_total + jnp.dot(
                    window, piece[time_tap, row_tap, col_tap], preferred_element_type=jnp.float32
                )
    return running_total.reshape(frame_count, row_count, col_count, out_width).astype(jnp.bfloat16)


def on_device(
    hidden_states,
    first_gain,
    second_gain,
    query_weight,
    key_weight,
    value_weight,
    out_weight,
    conv_kernel,
):
    source = hidden_states.astype(jnp.float32)
    normed = normalize(source, first_gain).astype(jnp.bfloat16)
    attended = attend(normed, query_weight, key_weight, value_weight, out_weight)
    resid = source + attended.astype(jnp.float32)
    activated = jax.nn.silu(normalize(resid, second_gain)).astype(jnp.bfloat16)
    convolved = convolve(activated, conv_kernel)
    return (attended, convolved)


def solution(mesh):
    placed = (
        P(("groups", "tm"), "space", None, "chan"),
        P("chan"),
        P("chan"),
        P(),
        P(),
        P(),
        P(),
        P(None, None, None, "tm", "chan"),
    )
    return jax.shard_map(
        on_device,
        mesh=mesh,
        in_specs=placed,
        out_specs=(
            P(("groups", "tm"), "space", None, "chan"),
            P(("groups", "tm"), "space", None, "chan"),
        ),
        check_vma=False,
    )
```

profile of v0, /device:TPU:0, one launch (start us, length us, event | category | flops | bytes accessed | tf_op | source)
XLA Modules:
  0.0 143.7 jit_solution(14035605134556565551)
XLA Ops:
  7.2 0.7 all-gather.2.cloned.1.call-update
  7.9 0.9 convert_reduce_fusion
  9.2 23.3 %all-reduce.2 = (f32[16]{0:T(128)S(1)}, f32[16]{0:T(128)S(1)}) all-reduce(f32[16]{0:T(128)S(1)} %reduce_sum.62, f32[16]{0:T(128)S(1)} %reduce_sum.59), channel_id=1, replica_groups=mesh['groups'=2,'space'=4,'tm'=2,'chan'=2] {'space','tm'}, use_global_device_ids=true, to_apply=%region_5.0 | all-reduce | flops 32 | bytes 256 | tf_op jit(solution)/shard_map/psum | solution.py:39
  32.9 0.9 fusion.26
  33.7 3.8 %all_to_all.35 = bf16[2,64,256]{2,1,0:T(8,128)(2,1)S(1)} all-to-all(bf16[2,64,256]{2,1,0:T(8,128)(2,1)S(1)} %fusion.26), channel_id=1, replica_groups=mesh['groups'=2,'space'=4,'tm'=2,'chan'=2] {'chan'}, dimensions={0} | all-to-all | bytes 131072 | tf_op jit(solution)/shard_map/all_to_all | solution.py:53
  37.5 0.2 convolution_convert_fusion.2
  37.8 14.3 %all_gather.12 = bf16[256,512]{1,0:T(8,128)(2,1)S(1)} all-gather(bf16[64,512]{1,0:T(8,128)(2,1)S(1)} %convolution_convert_fusion.2), channel_id=1, replica_groups=mesh['groups'=2,'space'=4,'tm'=2,'chan'=2] {'space'}, dimensions={0}, use_global_device_ids=true | all-gather | bytes 327680 | tf_op jit(solution)/shard_map/all_gather | solution.py:60
  52.1 1.2 convolution_convert_fusion.1
  53.3 13.9 %all_gather.13 = bf16[256,512]{1,0:T(8,128)(2,1)S(1)} all-gather(bf16[64,512]{1,0:T(8,128)(2,1)S(1)} %convolution_convert_fusion.1), channel_id=1, replica_groups=mesh['groups'=2,'space'=4,'tm'=2,'chan'=2] {'space'}, dimensions={0}, use_global_device_ids=true | all-gather | bytes 327680 | tf_op jit(solution)/shard_map/all_gather | solution.py:61
  67.2 1.5 %fusion.37 = (f32[64]{0:T(128)S(1)}, f32[64,256]{1,0:T(8,128)S(1)}) fusion(bf16[256,512]{1,0:T(8,128)(2,1)S(1)} %all_gather.12, bf16[64,512]{1,0:T(8,128)(2,1)S(1)} %bitcast.164, bf16[512,512]{1,0:T(8,128)(2,1)} %param.11), kind=kOutput, calls=%fused_computation.104 | convolution fusion | flops 50397120 | bytes 917760 | tf_op jit(solution)/shard_map/dot_general | solution.py:62
  68.9 1.4 convolution_convert_fusion
  70.3 3.8 %all_to_all.36 = bf16[64,2,256]{2,0,1:T(8,128)(2,1)S(1)} all-to-all(bf16[64,2,256]{2,0,1:T(8,128)(2,1)S(1)} %bitcast.193), channel_id=1, replica_groups=mesh['groups'=2,'space'=4,'tm'=2,'chan'=2] {'chan'}, dimensions={1} | all-to-all | bytes 131072 | tf_op jit(solution)/shard_map/all_to_all | solution.py:71
  74.6 17.4 %all-reduce.1 = (f32[16]{0:T(128)S(1)}, f32[16]{0:T(128)S(1)}) all-reduce(f32[16]{0:T(128)S(1)} %reduce_sum.85, f32[16]{0:T(128)S(1)} %reduce_sum.82), channel_id=1, replica_groups=mesh['groups'=2,'space'=4,'tm'=2,'chan'=2] {'space','tm'}, use_global_device_ids=true, to_apply=%region_13.14 | all-reduce | flops 32 | bytes 256 | tf_op jit(solution)/shard_map/psum | solution.py:39
  92.4 1.9 %all_gather.14 = bf16[2,1,64,512]{3,2,1,0:T(8,128)(2,1)S(1)} all-gather(bf16[2,1,64,256]{3,2,1,0:T(8,128)(2,1)S(1)} %multiply_convert_fusion), channel_id=1, replica_groups=mesh['groups'=2,'space'=4,'tm'=2,'chan'=2] {'chan'}, dimensions={3}, use_global_device_ids=true | all-gather | bytes 196608 | tf_op jit(solution)/shard_map/all_gather | solution.py:76
  94.3 4.1 %collective-permute-start = (bf16[2,1,64,512]{3,2,1,0:T(8,128)(2,1)S(1)}, bf16[2,1,64,512]{3,2,1,0:T(8,128)(2,1)S(1)}, u32[]{:S(2)}, u32[]{:S(2)}) collective-permute-start(bf16[2,1,64,512]{3,2,1,0:T(8,128)(2,1)S(1)} %all_gather.14), channel_id=1, source_target_pairs={{0,2},{1,3},{4,6},{5,7},{8,10},{9,11},{12,14},{13,15},{16,18},{17,... | collective-permute-start | bytes 393224 | tf_op jit(solution)/shard_map/ppermute | solution.py:14
  98.4 4.3 %collective-permute-done = bf16[2,1,64,512]{3,2,1,0:T(8,128)(2,1)S(1)} collective-permute-done((bf16[2,1,64,512]{3,2,1,0:T(8,128)(2,1)S(1)}, bf16[2,1,64,512]{3,2,1,0:T(8,128)(2,1)S(1)}, u32[]{:S(2)}, u32[]{:S(2)}) %collective-permute-start) | collective-permute-done | bytes 131104 | tf_op jit(solution)/shard_map/ppermute | solution.py:14
  102.8 3.0 %collective-permute-start.1 = (bf16[4,1,64,512]{3,2,1,0:T(8,128)(2,1)S(1)}, bf16[4,1,64,512]{3,2,1,0:T(8,128)(2,1)S(1)}, u32[]{:S(2)}, u32[]{:S(2)}) collective-permute-start(bf16[4,1,64,512]{3,2,1,0:T(8,128)(2,1)S(1)} %constant_dynamic-update-slice_fusion), channel_id=1, source_target_pairs={{0,4},{4,8},{8,12},{1,5},{5,9},{9,13},{2,6},{6,10},{10,14},{3,7},{... | collective-permute-start | bytes 786440 | tf_op jit(solution)/shard_map/ppermute | solution.py:25
  105.8 1.3 collective-permute-start.2
  107.1 3.8 %collective-permute-done.1 = bf16[4,1,64,512]{3,2,1,0:T(8,128)(2,1)S(1)} collective-permute-done((bf16[4,1,64,512]{3,2,1,0:T(8,128)(2,1)S(1)}, bf16[4,1,64,512]{3,2,1,0:T(8,128)(2,1)S(1)}, u32[]{:S(2)}, u32[]{:S(2)}) %collective-permute-start.1) | collective-permute-done | bytes 262176 | tf_op jit(solution)/shard_map/ppermute | solution.py:25
  110.9 4.1 %collective-permute-done.2 = bf16[4,1,64,512]{3,2,1,0:T(8,128)(2,1)S(1)} collective-permute-done((bf16[4,1,64,512]{3,2,1,0:T(8,128)(2,1)S(1)}, bf16[4,1,64,512]{3,2,1,0:T(8,128)(2,1)S(1)}, u32[]{:S(2)}, u32[]{:S(2)}) %collective-permute-start.2) | collective-permute-done | bytes 262176 | tf_op jit(solution)/shard_map/ppermute | solution.py:27
  115.0 0.2 fusion.13
  115.3 0.7 fusion.36
  116.0 0.8 fusion.35
  116.8 0.4 fusion.34
  117.2 1.3 fusion.20
  118.5 1.7 %fusion.19 = f32[128,256]{1,0:T(8,128)S(1)} fusion(bf16[128,512]{1,0:T(8,128)(2,1)S(1)} %bitcast.184, bf16[3,3,3,512,256]{4,3,2,1,0:T(8,128)(2,1)} %all-gather.2.cloned.1.call-done), kind=kOutput, calls=%fused_computation.69 | convolution fusion | flops 33554432 | bytes 524288 | tf_op jit(solution)/shard_map/dot_general | solution.py:102
  120.2 1.1 fusion.18
  121.4 1.1 fusion.17
  122.5 1.1 fusion.16
  123.7 1.2 fusion.15
  124.8 1.1 fusion.14
  126.0 1.1 convolution_add_fusion.19
  127.1 1.1 convolution_add_fusion.18
  128.3 1.1 convolution_add_fusion.17
  129.4 1.1 fusion.6
  130.6 1.1 convolution_add_fusion.15
  131.7 1.1 fusion.5
  133.0 0.2 fusion.4
  133.2 0.2 convolution_add_fusion.11
  133.4 0.2 convolution_add_fusion.10
  133.6 0.2 convolution_add_fusion.9
  134.0 0.2 fusion.3
  134.2 0.2 convolution_add_fusion.6
  134.4 0.2 fusion.2
  134.6 0.2 convolution_add_fusion.4
  135.0 0.2 convolution_add_fusion.2
  135.4 0.8 fusion.8
  136.3 0.6 copy.24
  (49 shorter events, 2.6 us)
Async XLA Ops:
  7.2 30.4 %copy-start = (bf16[512,512]{1,0:T(8,128)(2,1)S(1)}, bf16[512,512]{1,0:T(8,128)(2,1)}, u32[]{:S(2)}) copy-start(bf16[512,512]{1,0:T(8,128)(2,1)} %param.12) | copy-start | bytes 1572868
  7.2 67.0 %copy-start.2 = (bf16[2,1,64,256]{3,2,1,0:T(8,128)(2,1)S(1)}, bf16[2,1,64,256]{3,2,1,0:T(8,128)(2,1)}, u32[]{:S(2)}) copy-start(bf16[2,1,64,256]{3,2,1,0:T(8,128)(2,1)} %param.8) | copy-start | bytes 196612
  7.2 85.1 %copy-start.7 = (f32[256]{0:T(256)S(1)}, f32[256]{0:T(256)}, u32[]{:S(2)}) copy-start(f32[256]{0:T(256)} %param.10) | copy-start | bytes 3076
  7.2 110.0 %all-gather.2.cloned.1.call-start = ((), (), s32[]{:S(2)}) async-start(), calls=%async_computation.2 | async-start | bytes 10616832 | tf_op jit(solution)/shard_map/all_gather | solution.py:92
  94.3 8.4 %collective-permute-start = (bf16[2,1,64,512]{3,2,1,0:T(8,128)(2,1)S(1)}, bf16[2,1,64,512]{3,2,1,0:T(8,128)(2,1)S(1)}, u32[]{:S(2)}, u32[]{:S(2)}) collective-permute-start(bf16[2,1,64,512]{3,2,1,0:T(8,128)(2,1)S(1)} %all_gather.14), channel_id=1, source_target_pairs={{0,2},{1,3},{4,6},{5,7},{8,10},{9,11},{12,14},{13,15},{16,18},{17,... | collective-permute-start | bytes 393224 | tf_op jit(solution)/shard_map/ppermute | solution.py:14
  102.8 8.1 %collective-permute-start.1 = (bf16[4,1,64,512]{3,2,1,0:T(8,128)(2,1)S(1)}, bf16[4,1,64,512]{3,2,1,0:T(8,128)(2,1)S(1)}, u32[]{:S(2)}, u32[]{:S(2)}) collective-permute-start(bf16[4,1,64,512]{3,2,1,0:T(8,128)(2,1)S(1)} %constant_dynamic-update-slice_fusion), channel_id=1, source_target_pairs={{0,4},{4,8},{8,12},{1,5},{5,9},{9,13},{2,6},{6,10},{10,14},{3,7},{... | collective-permute-start | bytes 786440 | tf_op jit(solution)/shard_map/ppermute | solution.py:25
  105.8 9.2 %collective-permute-start.2 = (bf16[4,1,64,512]{3,2,1,0:T(8,128)(2,1)S(1)}, bf16[4,1,64,512]{3,2,1,0:T(8,128)(2,1)S(1)}, u32[]{:S(2)}, u32[]{:S(2)}) collective-permute-start(bf16[4,1,64,512]{3,2,1,0:T(8,128)(2,1)S(1)} %constant_dynamic-update-slice_fusion), channel_id=1, source_target_pairs={{4,0},{8,4},{12,8},{5,1},{9,5},{13,9},{6,2},{10,6},{14,10},{7,3},{... | collective-permute-start | bytes 786440 | tf_op jit(solution)/shard_map/ppermute | solution.py:27
  117.2 14.5 %copy-start.1 = (bf16[3,3,3,512,256]{4,3,2,1,0:T(8,128)(2,1)S(1)}, bf16[3,3,3,512,256]{4,3,2,1,0:T(8,128)(2,1)}, u32[]{:S(2)}) copy-start(bf16[3,3,3,512,256]{4,3,2,1,0:T(8,128)(2,1)} %all-gather.2.cloned.1.call-done) | copy-start | bytes 21233668
  117.2 15.8 %copy-start.6 = (bf16[2,1,64,512]{3,2,1,0:T(8,128)(2,1)S(1)}, bf16[2,1,64,512]{3,2,1,0:T(8,128)(2,1)}, u32[]{:S(2)}) copy-start(bf16[2,1,64,512]{3,2,1,0:T(8,128)(2,1)} %get-tuple-element.38) | copy-start | bytes 393220
  117.2 16.8 %copy-start.5 = (bf16[2,1,64,512]{3,2,1,0:T(8,128)(2,1)S(1)}, bf16[2,1,64,512]{3,2,1,0:T(8,128)(2,1)}, u32[]{:S(2)}) copy-start(bf16[2,1,64,512]{3,2,1,0:T(8,128)(2,1)} %get-tuple-element.35) | copy-start | bytes 393220
  117.2 17.2 %copy-start.4 = (bf16[2,1,64,512]{3,2,1,0:T(8,128)(2,1)S(1)}, bf16[2,1,64,512]{3,2,1,0:T(8,128)(2,1)}, u32[]{:S(2)}) copy-start(bf16[2,1,64,512]{3,2,1,0:T(8,128)(2,1)} %get-tuple-element.37) | copy-start | bytes 393220
  123.6 11.8 %copy-start.3 = (bf16[2,1,64,512]{3,2,1,0:T(8,128)(2,1)S(1)}, bf16[2,1,64,512]{3,2,1,0:T(8,128)(2,1)}, u32[]{:S(2)}) copy-start(bf16[2,1,64,512]{3,2,1,0:T(8,128)(2,1)} %get-tuple-element.34) | copy-start | bytes 393220
Sparse Core Ops, SparseCore 0:
  9.6 92.6 all-gather.1
where the time goes:
time: 145 us; the launch traced here: 144 us
  blocking collectives  78.5 us (54%)
  matrix products  23.1 us (16%)
  between operations  14.5 us (10%)
  waiting for transfers between devices  12.9 us (9%)
  starting transfers between devices  8.43 us (6%)
  local copies, waits for them, and re-layouts  3.52 us (2%)
  other arithmetic  2.8 us (2%)
    psum x2, blocking collectives, normalize(): lax.psum((jnp.sum(grouped, axis=(0, 2)), jnp.sum(grouped * grouped, axis=...  40.8 us
    dot_general x27, matrix products, convolve(): jnp.dot(window, piece[time_tap, row_tap, col_tap], preferred_element_type...  18.8 us
    all_gather x1, blocking collectives, attend(): key_piece = lax.all_gather(keyed, 'space', axis=0, tiled=True)  14.3 us
    all_gather x1, blocking collectives, attend(): value_piece = lax.all_gather(valued, 'space', axis=0, tiled=True)  13.9 us
    ppermute x1, waiting for transfers between devices, shifted_2(): return lax.ppermute(x, axis, pairs)  4.29 us
    ppermute x1, waiting for transfers between devices, padded_2(): lax.ppermute(head, axis, [((i + 1) % count, i) for i in range(ends)])  4.13 us
    ppermute x1, starting transfers between devices, shifted_2(): return lax.ppermute(x, axis, pairs)  4.12 us
    ppermute x1, waiting for transfers between devices, padded_2(): lax.ppermute(tail, axis, [(i, (i + 1) % count) for i in range(ends)])  3.8 us
  transfers between devices with their start and end apart: 4, of which 3 were waited for; matrix products, arithmetic and copies ran while one was open for 7% of the time, Pallas kernels for 0%

commit v1 on v0

--- a/solution.py
+++ b/solution.py
@@ -37,7 +37,8 @@
     grouped = source.reshape(-1, channels // group_width, group_width)
     population = grouped.shape[0] * group_width * lax.axis_size("space") * lax.axis_size("tm")
     group_sums, group_squares = lax.psum(
-        (jnp.sum(grouped, axis=(0, 2)), jnp.sum(grouped * grouped, axis=(0, 2))), ("space", "tm")
+        lax.psum((jnp.sum(grouped, axis=(0, 2)), jnp.sum(grouped * grouped, axis=(0, 2))), "tm"),
+        "space",
     )
     centre = group_sums / population
     spread = jnp.maximum(group_squares / population - centre * centre, 0.0)

time: 145 us -> 138 us (0.952)
  blocking collectives: 78.5 us -> 70.1 us
  waiting for transfers between devices: 12.9 us -> 15.1 us
    psum x2, blocking collectives: 40.8 us -> 11 us  [normalize(): lax.psum((jnp.sum(grouped, axis=(0, 2)), jnp.sum(grouped * grouped, axis=...]
    psum x0 -> x2, blocking collectives: none -> 21.4 us  [normalize(): lax.psum(lax.psum((jnp.sum(grouped, axis=(0, 2)), jnp.sum(grouped * group...]
    ppermute x1, waiting for transfers between devices: 4.29 us -> 6.44 us  [shifted_2(): return lax.ppermute(x, axis, pairs)]
where the time goes in v1:
time: 138 us; the launch traced here: 137 us
  blocking collectives  70.1 us (51%)
  matrix products  23.1 us (17%)
  waiting for transfers between devices  15.1 us (11%)
  between operations  14.5 us (11%)
  starting transfers between devices  8.07 us (6%)
  local copies, waits for them, and re-layouts  3.52 us (3%)
  other arithmetic  2.81 us (2%)
    psum x2, blocking collectives, normalize(): lax.psum(lax.psum((jnp.sum(grouped, axis=(0, 2)), jnp.sum(grouped * group...  21.4 us
    dot_general x27, matrix products, convolve(): jnp.dot(window, piece[time_tap, row_tap, col_tap], preferred_element_type...  18.8 us
    all_gather x1, blocking collectives, attend(): key_piece = lax.all_gather(keyed, 'space', axis=0, tiled=True)  14.3 us
    all_gather x1, blocking collectives, attend(): value_piece = lax.all_gather(valued, 'space', axis=0, tiled=True)  13.9 us
    psum x2, blocking collectives, normalize(): lax.psum((jnp.sum(grouped, axis=(0, 2)), jnp.sum(grouped * grouped, axis=...  11 us
    ppermute x1, waiting for transfers between devices, shifted_2(): return lax.ppermute(x, axis, pairs)  6.44 us
    ppermute x1, waiting for transfers between devices, padded_2(): lax.ppermute(head, axis, [((i + 1) % count, i) for i in range(ends)])  4.13 us
    ppermute x1, waiting for transfers between devices, padded_2(): lax.ppermute(tail, axis, [(i, (i + 1) % count) for i in range(ends)])  3.8 us
  transfers between devices with their start and end apart: 4, of which 3 were waited for; matrix products, arithmetic and copies ran while one was open for 7% of the time, Pallas kernels for 0%

profile of v1, /device:TPU:0, one launch (start us, length us, event | category | flops | bytes accessed | tf_op | source)
XLA Modules:
  0.0 137.2 jit_solution(8726998503000692527)
XLA Ops:
  7.2 0.7 all-gather.2.cloned.1.call-update
  7.9 0.9 convert_reduce_fusion
  9.2 5.9 %all-reduce.4 = (f32[16]{0:T(128)S(1)}, f32[16]{0:T(128)S(1)}) all-reduce(f32[16]{0:T(128)S(1)} %reduce_sum.62, f32[16]{0:T(128)S(1)} %reduce_sum.59), channel_id=1, replica_groups=mesh['groups'=2,'space'=4,'tm'=2,'chan'=2] {'tm'}, use_global_device_ids=true, to_apply=%region_6.0 | all-reduce | flops 32 | bytes 256 | tf_op jit(solution)/shard_map/psum | solution.py:40
  15.1 12.5 %all-reduce.2 = (f32[16]{0:T(128)S(1)}, f32[16]{0:T(128)S(1)}) all-reduce(f32[16]{0:T(128)S(1)} %get-tuple-element.18, f32[16]{0:T(128)S(1)} %get-tuple-element.19), channel_id=1, replica_groups=mesh['groups'=2,'space'=4,'tm'=2,'chan'=2] {'space'}, use_global_device_ids=true, to_apply=%region_7.0 | all-reduce | flops 32 | bytes 256 | tf_op jit(solution)/shard_map/psum | solution.py:39
  27.9 0.9 fusion.26
  28.8 3.8 %all_to_all.35 = bf16[2,64,256]{2,1,0:T(8,128)(2,1)S(1)} all-to-all(bf16[2,64,256]{2,1,0:T(8,128)(2,1)S(1)} %fusion.26), channel_id=1, replica_groups=mesh['groups'=2,'space'=4,'tm'=2,'chan'=2] {'chan'}, dimensions={0} | all-to-all | bytes 131072 | tf_op jit(solution)/shard_map/all_to_all | solution.py:54
  32.6 0.2 convolution_convert_fusion.2
  32.8 14.3 %all_gather.12 = bf16[256,512]{1,0:T(8,128)(2,1)S(1)} all-gather(bf16[64,512]{1,0:T(8,128)(2,1)S(1)} %convolution_convert_fusion.2), channel_id=1, replica_groups=mesh['groups'=2,'space'=4,'tm'=2,'chan'=2] {'space'}, dimensions={0}, use_global_device_ids=true | all-gather | bytes 327680 | tf_op jit(solution)/shard_map/all_gather | solution.py:61
  47.1 1.2 convolution_convert_fusion.1
  48.3 13.9 %all_gather.13 = bf16[256,512]{1,0:T(8,128)(2,1)S(1)} all-gather(bf16[64,512]{1,0:T(8,128)(2,1)S(1)} %convolution_convert_fusion.1), channel_id=1, replica_groups=mesh['groups'=2,'space'=4,'tm'=2,'chan'=2] {'space'}, dimensions={0}, use_global_device_ids=true | all-gather | bytes 327680 | tf_op jit(solution)/shard_map/all_gather | solution.py:62
  62.2 1.5 %fusion.37 = (f32[64]{0:T(128)S(1)}, f32[64,256]{1,0:T(8,128)S(1)}) fusion(bf16[256,512]{1,0:T(8,128)(2,1)S(1)} %all_gather.12, bf16[64,512]{1,0:T(8,128)(2,1)S(1)} %bitcast.164, bf16[512,512]{1,0:T(8,128)(2,1)} %param.11), kind=kOutput, calls=%fused_computation.104 | convolution fusion | flops 50397120 | bytes 917760 | tf_op jit(solution)/shard_map/dot_general | solution.py:63
  63.9 1.4 %convolution_convert_fusion = bf16[64,512]{1,0:T(8,128)(2,1)S(1)} fusion(bf16[512,512]{1,0:T(8,128)(2,1)} %param.14, bf16[256,512]{1,0:T(8,128)(2,1)S(1)} %all_gather.13, f32[64]{0:T(128)S(1)} %fusion.28, f32[64,256]{1,0:T(8,128)S(1)} %get-tuple-element.49, f32[64]{0:T(128)S(1)} %broadcast_maximum_fusion), kind=kOutput, calls=%fused_computation.32 | convolution fusion | flops 50462720 | bytes 918016 | tf_op jit(solution)/shard_map/dot_general | solution.py:71
  65.4 3.8 %all_to_all.36 = bf16[64,2,256]{2,0,1:T(8,128)(2,1)S(1)} all-to-all(bf16[64,2,256]{2,0,1:T(8,128)(2,1)S(1)} %bitcast.193), channel_id=1, replica_groups=mesh['groups'=2,'space'=4,'tm'=2,'chan'=2] {'chan'}, dimensions={1} | all-to-all | bytes 131072 | tf_op jit(solution)/shard_map/all_to_all | solution.py:72
  69.6 5.1 %all-reduce.3 = (f32[16]{0:T(128)S(1)}, f32[16]{0:T(128)S(1)}) all-reduce(f32[16]{0:T(128)S(1)} %reduce_sum.85, f32[16]{0:T(128)S(1)} %reduce_sum.82), channel_id=1, replica_groups=mesh['groups'=2,'space'=4,'tm'=2,'chan'=2] {'tm'}, use_global_device_ids=true, to_apply=%region_16.17 | all-reduce | flops 32 | bytes 256 | tf_op jit(solution)/shard_map/psum | solution.py:40
  74.7 8.9 %all-reduce.1 = (f32[16]{0:T(128)S(1)}, f32[16]{0:T(128)S(1)}) all-reduce(f32[16]{0:T(128)S(1)} %get-tuple-element.16, f32[16]{0:T(128)S(1)} %get-tuple-element.17), channel_id=1, replica_groups=mesh['groups'=2,'space'=4,'tm'=2,'chan'=2] {'space'}, use_global_device_ids=true, to_apply=%region_17.18 | all-reduce | flops 32 | bytes 256 | tf_op jit(solution)/shard_map/psum | solution.py:39
  84.0 1.9 %all_gather.14 = bf16[2,1,64,512]{3,2,1,0:T(8,128)(2,1)S(1)} all-gather(bf16[2,1,64,256]{3,2,1,0:T(8,128)(2,1)S(1)} %multiply_convert_fusion), channel_id=1, replica_groups=mesh['groups'=2,'space'=4,'tm'=2,'chan'=2] {'chan'}, dimensions={3}, use_global_device_ids=true | all-gather | bytes 196608 | tf_op jit(solution)/shard_map/all_gather | solution.py:77
  85.9 3.4 %collective-permute-start = (bf16[2,1,64,512]{3,2,1,0:T(8,128)(2,1)S(1)}, bf16[2,1,64,512]{3,2,1,0:T(8,128)(2,1)S(1)}, u32[]{:S(2)}, u32[]{:S(2)}) collective-permute-start(bf16[2,1,64,512]{3,2,1,0:T(8,128)(2,1)S(1)} %all_gather.14), channel_id=1, source_target_pairs={{0,2},{1,3},{4,6},{5,7},{8,10},{9,11},{12,14},{13,15},{16,18},{17,... | collective-permute-start | bytes 393224 | tf_op jit(solution)/shard_map/ppermute | solution.py:14
  89.3 6.4 %collective-permute-done = bf16[2,1,64,512]{3,2,1,0:T(8,128)(2,1)S(1)} collective-permute-done((bf16[2,1,64,512]{3,2,1,0:T(8,128)(2,1)S(1)}, bf16[2,1,64,512]{3,2,1,0:T(8,128)(2,1)S(1)}, u32[]{:S(2)}, u32[]{:S(2)}) %collective-permute-start) | collective-permute-done | bytes 131104 | tf_op jit(solution)/shard_map/ppermute | solution.py:14
  95.8 3.3 %collective-permute-start.1 = (bf16[4,1,64,512]{3,2,1,0:T(8,128)(2,1)S(1)}, bf16[4,1,64,512]{3,2,1,0:T(8,128)(2,1)S(1)}, u32[]{:S(2)}, u32[]{:S(2)}) collective-permute-start(bf16[4,1,64,512]{3,2,1,0:T(8,128)(2,1)S(1)} %constant_dynamic-update-slice_fusion), channel_id=1, source_target_pairs={{0,4},{4,8},{8,12},{1,5},{5,9},{9,13},{2,6},{6,10},{10,14},{3,7},{... | collective-permute-start | bytes 786440 | tf_op jit(solution)/shard_map/ppermute | solution.py:25
  99.2 1.3 collective-permute-start.2
  100.5 3.8 %collective-permute-done.1 = bf16[4,1,64,512]{3,2,1,0:T(8,128)(2,1)S(1)} collective-permute-done((bf16[4,1,64,512]{3,2,1,0:T(8,128)(2,1)S(1)}, bf16[4,1,64,512]{3,2,1,0:T(8,128)(2,1)S(1)}, u32[]{:S(2)}, u32[]{:S(2)}) %collective-permute-start.1) | collective-permute-done | bytes 262176 | tf_op jit(solution)/shard_map/ppermute | solution.py:25
  104.3 4.1 %collective-permute-done.2 = bf16[4,1,64,512]{3,2,1,0:T(8,128)(2,1)S(1)} collective-permute-done((bf16[4,1,64,512]{3,2,1,0:T(8,128)(2,1)S(1)}, bf16[4,1,64,512]{3,2,1,0:T(8,128)(2,1)S(1)}, u32[]{:S(2)}, u32[]{:S(2)}) %collective-permute-start.2) | collective-permute-done | bytes 262176 | tf_op jit(solution)/shard_map/ppermute | solution.py:27
  108.4 0.2 fusion.13
  108.7 0.7 fusion.36
  109.4 0.8 fusion.35
  110.2 0.4 fusion.34
  110.6 1.3 fusion.20
  111.9 1.7 %fusion.19 = f32[128,256]{1,0:T(8,128)S(1)} fusion(bf16[128,512]{1,0:T(8,128)(2,1)S(1)} %bitcast.184, bf16[3,3,3,512,256]{4,3,2,1,0:T(8,128)(2,1)} %all-gather.2.cloned.1.call-done), kind=kOutput, calls=%fused_computation.69 | convolution fusion | flops 33554432 | bytes 524288 | tf_op jit(solution)/shard_map/dot_general | solution.py:103
  113.6 1.1 fusion.18
  114.8 1.1 fusion.17
  115.9 1.1 fusion.16
  117.1 1.2 fusion.15
  118.2 1.1 fusion.14
  119.4 1.1 convolution_add_fusion.19
  120.5 1.1 convolution_add_fusion.18
  121.7 1.1 convolution_add_fusion.17
  122.8 1.1 fusion.6
  124.0 1.1 convolution_add_fusion.15
  125.1 1.1 fusion.5
  126.4 0.2 fusion.4
  126.6 0.2 convolution_add_fusion.11
  127.0 0.2 convolution_add_fusion.9
  127.4 0.2 fusion.3
  127.6 0.2 convolution_add_fusion.6
  128.1 0.2 convolution_add_fusion.4
  128.4 0.2 convolution_add_fusion.2
  128.9 0.8 fusion.8
  129.7 0.6 copy.24
  (51 shorter events, 3.0 us)
Async XLA Ops:
  7.2 25.4 %copy-start = (bf16[512,512]{1,0:T(8,128)(2,1)S(1)}, bf16[512,512]{1,0:T(8,128)(2,1)}, u32[]{:S(2)}) copy-start(bf16[512,512]{1,0:T(8,128)(2,1)} %param.12) | copy-start | bytes 1572868
  7.2 62.0 %copy-start.2 = (bf16[2,1,64,256]{3,2,1,0:T(8,128)(2,1)S(1)}, bf16[2,1,64,256]{3,2,1,0:T(8,128)(2,1)}, u32[]{:S(2)}) copy-start(bf16[2,1,64,256]{3,2,1,0:T(8,128)(2,1)} %param.8) | copy-start | bytes 196612
  7.2 76.8 %copy-start.7 = (f32[256]{0:T(256)S(1)}, f32[256]{0:T(256)}, u32[]{:S(2)}) copy-start(f32[256]{0:T(256)} %param.10) | copy-start | bytes 3076
  7.2 103.4 %all-gather.2.cloned.1.call-start = ((), (), s32[]{:S(2)}) async-start(), calls=%async_computation.2 | async-start | bytes 10616832 | tf_op jit(solution)/shard_map/all_gather | solution.py:93
  85.9 9.9 %collective-permute-start = (bf16[2,1,64,512]{3,2,1,0:T(8,128)(2,1)S(1)}, bf16[2,1,64,512]{3,2,1,0:T(8,128)(2,1)S(1)}, u32[]{:S(2)}, u32[]{:S(2)}) collective-permute-start(bf16[2,1,64,512]{3,2,1,0:T(8,128)(2,1)S(1)} %all_gather.14), channel_id=1, source_target_pairs={{0,2},{1,3},{4,6},{5,7},{8,10},{9,11},{12,14},{13,15},{16,18},{17,... | collective-permute-start | bytes 393224 | tf_op jit(solution)/shard_map/ppermute | solution.py:14
  95.8 8.5 %collective-permute-start.1 = (bf16[4,1,64,512]{3,2,1,0:T(8,128)(2,1)S(1)}, bf16[4,1,64,512]{3,2,1,0:T(8,128)(2,1)S(1)}, u32[]{:S(2)}, u32[]{:S(2)}) collective-permute-start(bf16[4,1,64,512]{3,2,1,0:T(8,128)(2,1)S(1)} %constant_dynamic-update-slice_fusion), channel_id=1, source_target_pairs={{0,4},{4,8},{8,12},{1,5},{5,9},{9,13},{2,6},{6,10},{10,14},{3,7},{... | collective-permute-start | bytes 786440 | tf_op jit(solution)/shard_map/ppermute | solution.py:25
  99.2 9.2 %collective-permute-start.2 = (bf16[4,1,64,512]{3,2,1,0:T(8,128)(2,1)S(1)}, bf16[4,1,64,512]{3,2,1,0:T(8,128)(2,1)S(1)}, u32[]{:S(2)}, u32[]{:S(2)}) collective-permute-start(bf16[4,1,64,512]{3,2,1,0:T(8,128)(2,1)S(1)} %constant_dynamic-update-slice_fusion), channel_id=1, source_target_pairs={{4,0},{8,4},{12,8},{5,1},{9,5},{13,9},{6,2},{10,6},{14,10},{7,3},{... | collective-permute-start | bytes 786440 | tf_op jit(solution)/shard_map/ppermute | solution.py:27
  110.6 14.5 %copy-start.1 = (bf16[3,3,3,512,256]{4,3,2,1,0:T(8,128)(2,1)S(1)}, bf16[3,3,3,512,256]{4,3,2,1,0:T(8,128)(2,1)}, u32[]{:S(2)}) copy-start(bf16[3,3,3,512,256]{4,3,2,1,0:T(8,128)(2,1)} %all-gather.2.cloned.1.call-done) | copy-start | bytes 21233668
  110.6 15.8 %copy-start.6 = (bf16[2,1,64,512]{3,2,1,0:T(8,128)(2,1)S(1)}, bf16[2,1,64,512]{3,2,1,0:T(8,128)(2,1)}, u32[]{:S(2)}) copy-start(bf16[2,1,64,512]{3,2,1,0:T(8,128)(2,1)} %get-tuple-element.42) | copy-start | bytes 393220
  110.6 16.8 %copy-start.5 = (bf16[2,1,64,512]{3,2,1,0:T(8,128)(2,1)S(1)}, bf16[2,1,64,512]{3,2,1,0:T(8,128)(2,1)}, u32[]{:S(2)}) copy-start(bf16[2,1,64,512]{3,2,1,0:T(8,128)(2,1)} %get-tuple-element.39) | copy-start | bytes 393220
  110.6 17.2 %copy-start.4 = (bf16[2,1,64,512]{3,2,1,0:T(8,128)(2,1)S(1)}, bf16[2,1,64,512]{3,2,1,0:T(8,128)(2,1)}, u32[]{:S(2)}) copy-start(bf16[2,1,64,512]{3,2,1,0:T(8,128)(2,1)} %get-tuple-element.41) | copy-start | bytes 393220
  117.1 11.8 %copy-start.3 = (bf16[2,1,64,512]{3,2,1,0:T(8,128)(2,1)S(1)}, bf16[2,1,64,512]{3,2,1,0:T(8,128)(2,1)}, u32[]{:S(2)}) copy-start(bf16[2,1,64,512]{3,2,1,0:T(8,128)(2,1)} %get-tuple-element.38) | copy-start | bytes 393220
Sparse Core Ops, SparseCore 0:
  9.6 92.5 all-gather.1
